TPU v7x, 256 devices: a whole 4x4x8 slice. The times are simulated.
256 devices in a mesh: inner: 8 (over x, core), outer: 32 (over z, y).
Axes of the slice: x: 4, y: 4, z: 8, core: 2. Of those that a mesh axis runs over, the one named last changes fastest.
Arguments:
- queries: bfloat16 [32768, 2048], P(('outer', 'inner')), may hold values from -6 to 6
- keys: bfloat16 [32768, 2048], P(('outer', 'inner')), may hold values from -6 to 6
- values: bfloat16 [32768, 2048], P(('outer', 'inner')), may hold values from -6 to 6
- out_grad: bfloat16 [32768, 2048], P(('outer', 'inner')), may hold values from -6 to 6
- positions: int32 [32768], P(('outer', 'inner')), may hold values from 0 to 8191
Outputs:
- attended: bfloat16 [32768, 2048], P(('outer', 'inner'))
- query_grad: bfloat16 [32768, 2048], P(('outer', 'inner'))
- key_grad: bfloat16 [32768, 2048], P(('outer', 'inner'))
- value_gradient: bfloat16 [32768, 2048], P(('outer', 'inner'))
All inputs are finite; a program needn't handle non-finite values.
Results may differ from a plain program's by a relative error of at most 0.0064.
Values sent between devices are 32-bit elements; how exact they have to be, the bound alone decides.
A program may use at most 256 MiB of HBM per device.

v0:
```python
import math
import jax
import jax.numpy as jnp
from jax import lax
from jax.sharding import PartitionSpec as P

D_HEAD = 128


def carried_in(value, axis, join, neutral, backward):
    count, mine = (lax.axis_size(axis), lax.axis_index(axis))
    pieces = lax.all_gather(value, axis)
    if backward:
        pieces = pieces[::-1]
        mine = count - 1 - mine
    so_far = jnp.full_like(value, 0) + jnp.asarray(neutral, value.dtype)

    def step(position, so_far):
        longer = join(so_far, pieces[position])
        return jnp.where(position < mine, longer, so_far)

    return lax.fori_loop(0, count - 1, step, so_far)


def rotary_tables(positions, head_dim):
    half_dim = head_dim // 2
    spacing = jnp.arange(half_dim).astype(jnp.float32) * (-2.0 * math.log(500000.0) / head_dim)
    angle = positions.astype(jnp.float32)[:, None] * jnp.exp(spacing)[None, :]
    return (jnp.cos(angle)[:, None, :], jnp.sin(angle)[:, None, :])


def rotate(rows, cosine, sine):
    half_dim = rows.shape[-1] // 2
    first = rows[..., :half_dim].astype(jnp.float32)
    second = rows[..., half_dim:].astype(jnp.float32)
    return jnp.concatenate(
        [first * cosine - second * sine, second * cosine + first * sine], axis=-1
    )


def unrotate(rows, cosine, sine):
    half_dim = rows.shape[-1] // 2
    first = rows[..., :half_dim]
    second = rows[..., half_dim:]
    return jnp.concatenate(
        [first * cosine + second * sine, second * cosine - first * sine], axis=-1
    )


def add_states(earlier, later):
    return earlier + later


def outer_sums(keys_group, queries_group):
    zero_part = jnp.zeros_like(keys_group)
    keys_earlier = carried_in(keys_group, "outer", add_states, zero_part, False)
    queries_later = carried_in(queries_group, "outer", add_states, zero_part, True)
    return (keys_earlier, queries_later)


def shards(queries, keys, values, out_grad, positions):
    rows_here = queries.shape[0]
    head_dim = D_HEAD
    heads_count = queries.shape[1] // head_dim
    total_tokens = rows_here * lax.axis_size("inner") * lax.axis_size("outer")
    scale_factor = (head_dim * total_tokens) ** (-0.5)
    cosine, sine = rotary_tables(positions, head_dim)
    shaped = (rows_here, heads_count, head_dim)
    rotated_query = rotate(queries.reshape(shaped), cosine, sine).astype(jnp.bfloat16)
    rotated_key = rotate(keys.reshape(shaped), cosine, sine).astype(jnp.bfloat16)
    value_row_block = values.reshape(shaped)
    gradient_row_block = out_grad.reshape(shaped)
    key_value_state = jnp.einsum(
        "pob,poj->obj", rotated_key, value_row_block, preferred_element_type=jnp.float32
    )
    query_state = jnp.einsum(
        "pob,poj->obj", rotated_query, gradient_row_block, preferred_element_type=jnp.float32
    )
    own_place = lax.axis_index("inner")
    piece = (
        lax.all_gather(key_value_state[None], "inner", axis=0, tiled=True),
        lax.all_gather(query_state[None], "inner", axis=0, tiled=True),
    )
    count = piece[0].shape[0]
    order = jnp.arange(count, dtype=jnp.int32)
    earlier = (order < own_place)[:, None, None, None]
    later = (order > own_place)[:, None, None, None]
    keys_before = jnp.sum(jnp.where(earlier, piece[0], 0.0), axis=0)
    queries_after = jnp.sum(jnp.where(later, piece[1], 0.0), axis=0)
    keys_group = jnp.sum(piece[0], axis=0)
    queries_group = jnp.sum(piece[1], axis=0)
    keys_earlier, queries_later = outer_sums(keys_group, queries_group)
    preceding_state = (keys_earlier + keys_before).astype(jnp.bfloat16)
    following_state = (queries_later + queries_after).astype(jnp.bfloat16)
    causal = (jnp.arange(rows_here)[:, None] >= jnp.arange(rows_here)[None, :])[None]
    score_matrix = jnp.where(
        causal,
        jnp.einsum("thd,shd->hts", rotated_query, rotated_key, preferred_element_type=jnp.float32),
        0.0,
    ).astype(jnp.bfloat16)
    score_gradient = jnp.where(
        causal,
        jnp.einsum(
            "thd,shd->hts", gradient_row_block, value_row_block, preferred_element_type=jnp.float32
        ),
        0.0,
    ).astype(jnp.bfloat16)
    attended = scale_factor * (
        jnp.einsum(
            "rgb,brf->grf", score_matrix, value_row_block, preferred_element_type=jnp.float32
        )
        + jnp.einsum(
            "axz,xzo->axo", rotated_query, preceding_state, preferred_element_type=jnp.float32
        )
    )
    rotated_query_gradient = scale_factor * (
        jnp.einsum("rgb,brf->grf", score_gradient, rotated_key, preferred_element_type=jnp.float32)
        + jnp.einsum(
            "xge,gme->xgm", gradient_row_block, preceding_state, preferred_element_type=jnp.float32
        )
    )
    rotated_key_gradient = scale_factor * (
        jnp.einsum(
            "uox,oul->xul", score_gradient, rotated_query, preferred_element_type=jnp.float32
        )
        + jnp.einsum(
            "olb,lfb->olf", value_row_block, following_state, preferred_element_type=jnp.float32
        )
    )
    value_gradient = scale_factor * (
        jnp.einsum(
            "uox,oul->xul", score_matrix, gradient_row_block, preferred_element_type=jnp.float32
        )
        + jnp.einsum(
            "tyg,yge->tye", rotated_key, following_state, preferred_element_type=jnp.float32
        )
    )
    flat = (rows_here, heads_count * head_dim)
    return (
        attended.astype(jnp.bfloat16).reshape(flat),
        unrotate(rotated_query_gradient, cosine, sine).astype(jnp.bfloat16).reshape(flat),
        unrotate(rotated_key_gradient, cosine, sine).astype(jnp.bfloat16).reshape(flat),
        value_gradient.astype(jnp.bfloat16).reshape(flat),
    )


def solution(mesh):
    placed = (
        P(("outer", "inner"), None),
        P(("outer", "inner"), None),
        P(("outer", "inner"), None),
        P(("outer", "inner"), None),
        P(("outer", "inner")),
    )
    return jax.shard_map(
        shards,
        mesh=mesh,
        in_specs=placed,
        out_specs=(
            P(("outer", "inner"), None),
            P(("outer", "inner"), None),
            P(("outer", "inner"), None),
            P(("outer", "inner"), None),
        ),
        check_vma=False,
    )
```

profile of v0, /device:TPU:1, one launch (start us, length us, event | category | flops | bytes accessed | tf_op | source)
XLA Modules:
  0.0 743.1 jit_solution(15101625095384080709)
XLA Ops:
  13.8 56.5 %all-gather.13.cloned.1.call-done = f32[128,128,128]{2,1,0:T(8,128)} async-done(((f32[16,128,128]{2,1,0:T(8,128)}), f32[128,128,128]{2,1,0:T(8,128)}) %all-gather.13.cloned.1.call-update) | async-done | bytes 8388624 | tf_op jit(solution)/shard_map/all_gather | solution.py:82
  70.3 6.1 select_reduce_fusion
  78.6 2.0 copy.101
  83.4 225.2 %all-gather.15.cloned.1.call-done = f32[512,128,128]{2,1,0:T(8,128)} async-done(((f32[16,128,128]{2,1,0:T(8,128)}), f32[512,128,128]{2,1,0:T(8,128)}) %all-gather.15.cloned.1.call-update) | async-done | bytes 33554448 | tf_op jit(solution)/shard_map/all_gather | solution.py:12
  308.6 23.0 %rev.3 = f32[32,16,128,128]{3,2,1,0:T(8,128)} reverse(f32[32,16,128,128]{3,2,1,0:T(8,128)} %bitcast.85), dimensions={0} | reverse | bytes 67108864 | tf_op jit(solution)/shard_map/rev | solution.py:14
  331.6 50.0 %while.29 = (s32[]{:T(128)}, f32[16,128,128]{2,1,0:T(8,128)S(1)}, s32[]{:T(128)}, f32[32,16,128,128]{3,2,1,0:T(8,128)}, s32[]{:T(128)}, /*index=5*/s32[]{:T(128)}) while((s32[]{:T(128)}, f32[16,128,128]{2,1,0:T(8,128)S(1)}, s32[]{:T(128)}, f32[32,16,128,128]{3,2,1,0:T(8,128)}, s32[]{:T(128)}, /*index=5*/s32[]{:T(128)}) %tuple.77), condition=%wide.region_6.7_spmd.clone, body=%wide.region_5.6_spmd.clone.sunk | while | flops 786436 | bytes 3145821 | solution.py:22
  333.2 1.6 add_select_fusion.5
  334.8 1.6 add_select_fusion.5
  339.7 1.6 add_select_fusion.5
  341.3 1.6 add_select_fusion.5
  342.9 1.6 add_select_fusion.5
  346.1 1.6 add_select_fusion.5
  347.7 1.6 add_select_fusion.5
  349.4 1.6 add_select_fusion.5
  351.0 1.6 add_select_fusion.5
  354.2 1.6 add_select_fusion.5
  355.8 1.6 add_select_fusion.5
  357.4 1.6 add_select_fusion.5
  362.3 1.6 add_select_fusion.5
  363.9 1.6 add_select_fusion.5
  365.5 1.6 add_select_fusion.5
  370.3 1.6 add_select_fusion.5
  371.9 1.6 add_select_fusion.5
  373.6 1.6 add_select_fusion.5
  376.8 1.6 add_select_fusion.5
  378.4 1.6 add_select_fusion.5
  380.0 1.6 add_select_fusion.5
  383.0 1.9 fusion.5
  384.9 2.6 add_convert_fusion
  389.5 50.3 %all-gather.9.cloned.1.call-done = f32[128,128,128]{2,1,0:T(8,128)} async-done(((f32[16,128,128]{2,1,0:T(8,128)}), f32[128,128,128]{2,1,0:T(8,128)}) %all-gather.9.cloned.1.call-update) | async-done | bytes 8388624 | tf_op jit(solution)/shard_map/all_gather | solution.py:81
  439.8 6.1 select_reduce_fusion.1
  446.4 1.7 convolution_bitcast_fusion.1
  449.3 2.0 copy.88
  451.3 2.3 pad_maximum_fusion.3
  453.6 2.0 copy.82
  455.7 2.0 copy.87
  457.7 2.6 convolution_bitcast_fusion.3
  460.3 217.8 %all-gather.11.cloned.1.call-done = f32[512,128,128]{2,1,0:T(8,128)} async-done(((f32[16,128,128]{2,1,0:T(8,128)}), f32[512,128,128]{2,1,0:T(8,128)}) %all-gather.11.cloned.1.call-update) | async-done | bytes 33554448 | tf_op jit(solution)/shard_map/all_gather | solution.py:12
  678.1 50.0 %while.28 = (s32[]{:T(128)}, f32[16,128,128]{2,1,0:T(8,128)S(1)}, s32[]{:T(128)}, f32[32,16,128,128]{3,2,1,0:T(8,128)}, s32[]{:T(128)}, /*index=5*/s32[]{:T(128)}) while((s32[]{:T(128)}, f32[16,128,128]{2,1,0:T(8,128)S(1)}, s32[]{:T(128)}, f32[32,16,128,128]{3,2,1,0:T(8,128)}, s32[]{:T(128)}, /*index=5*/s32[]{:T(128)}) %tuple.91), condition=%wide.region_2.3_spmd.clone, body=%wide.region_1.2_spmd.clone.sunk | while | flops 786436 | bytes 3145821 | solution.py:22
  679.7 1.6 add_select_fusion.4
  681.3 1.6 add_select_fusion.4
  682.9 1.6 add_select_fusion.4
  684.6 1.6 add_select_fusion.4
  686.2 1.6 add_select_fusion.4
  687.8 1.6 add_select_fusion.4
  691.0 1.6 add_select_fusion.4
  694.2 1.6 add_select_fusion.4
  733.7 1.9 fusion.8
  (85 shorter events, 75.5 us)
Async XLA Ops:
  7.2 74.4 %copy-start = (bf16[128,2048]{1,0:T(8,128)(2,1)S(1)}, bf16[128,2048]{1,0:T(8,128)(2,1)}, u32[]{:S(2)}) copy-start(bf16[128,2048]{1,0:T(8,128)(2,1)} %param.11) | copy-start | bytes 1572868
  7.2 63.1 %all-gather.13.cloned.1.call-start = ((), (), s32[]{:S(2)}) async-start(), calls=%async_computation.2 | async-start | bytes 9437184 | tf_op jit(solution)/shard_map/all_gather | solution.py:82
  13.8 294.8 %all-gather.15.cloned.1.call-start = ((), (), s32[]{:S(2)}) async-start(), calls=%async_computation.3 | async-start | bytes 34603008 | tf_op jit(solution)/shard_map/all_gather | solution.py:12
  76.4 363.4 %all-gather.9.cloned.1.call-start = ((), (), s32[]{:S(2)}) async-start(), calls=%async_computation | async-start | bytes 9437184 | tf_op jit(solution)/shard_map/all_gather | solution.py:81
  82.1 249.5 %copy-start.4 = (bf16[16,128,128]{2,1,0:T(8,128)(2,1)}, bf16[16,128,128]{2,1,0:T(8,128)(2,1)S(1)}, u32[]{:S(2)}) copy-start(bf16[16,128,128]{2,1,0:T(8,128)(2,1)S(1)} %fusion.11) | copy-start | bytes 1572868
  383.0 62.9 %copy-start.3 = (bf16[16,128,128]{2,1,0:T(8,128)(2,1)}, bf16[16,128,128]{2,1,0:T(8,128)(2,1)S(1)}, u32[]{:S(2)}) copy-start(bf16[16,128,128]{2,1,0:T(8,128)(2,1)S(1)} %add_convert_fusion.1) | copy-start | bytes 1572868
  389.2 288.8 %all-gather.11.cloned.1.call-start = ((), (), s32[]{:S(2)}) async-start(), calls=%async_computation.1 | async-start | bytes 34603008 | tf_op jit(solution)/shard_map/all_gather | solution.py:12
  446.4 1.8 copy-start.2
  729.5 0.8 copy-start.1
Sparse Core Ops, SparseCore 0:
  13.9 56.3 all-gather.12
  76.6 232.0 all-gather.14
  389.4 50.3 all-gather.8
  446.0 232.0 all-gather.10
where the time goes:
time: 746 us; the launch traced here: 743 us
  waiting for transfers between devices  550 us (74%)
  other arithmetic  121 us (16%)
  local copies, waits for them, and re-layouts  40 us (5%)
  matrix products  16.5 us (2%)
  between operations  14 us (2%)
    all_gather x2, waiting for transfers between devices, carried_in(): pieces = lax.all_gather(value, axis)  443 us
    select_n x62, other arithmetic, step(): return jnp.where(position < mine, longer, so_far)  98.5 us
    all_gather x1, waiting for transfers between devices, shards(): lax.all_gather(query_state[None], 'inner', axis=0, tiled=True)  56.5 us
    all_gather x1, waiting for transfers between devices, shards(): lax.all_gather(key_value_state[None], 'inner', axis=0, tiled=True)  50.3 us
    rev x1, local copies, waits for them, and re-layouts, carried_in(): pieces = pieces[::-1]  23 us
  transfers between devices with their start and end apart: 4, of which 4 were waited for; matrix products, arithmetic and copies ran while one was open for 3% of the time, Pallas kernels for 0%

commit v1 on v0

--- a/solution.py
+++ b/solution.py
@@ -5,6 +5,13 @@
 from jax.sharding import PartitionSpec as P
 
 D_HEAD = 128
+
+
+def _move_skins(buf):
+    latest = tuple((buf for _ in range(lax.axis_size("inner"))))
+    last = jnp.stack(latest, 0)
+    value_now = lax.all_to_all(last, concat_axis=0, axis_name="inner", split_axis=0)
+    return jnp.concatenate(value_now, 0)
 
 
 def carried_in(value, axis, join, neutral, backward):
@@ -79,7 +86,7 @@
     own_place = lax.axis_index("inner")
     piece = (
         lax.all_gather(key_value_state[None], "inner", axis=0, tiled=True),
-        lax.all_gather(query_state[None], "inner", axis=0, tiled=True),
+        _move_skins(query_state[None]),
     )
     count = piece[0].shape[0]
     order = jnp.arange(count, dtype=jnp.int32)

time: 746 us -> 790 us (1.059)
  blocking collectives: 0 us -> 100 us
  waiting for transfers between devices: 550 us -> 489 us
    all_to_all x0 -> x1, blocking collectives: none -> 100 us  [_move_skins(): lax.all_to_all(last, concat_axis=0, axis_name='inner', split_axis=0)]
    all_gather x1 -> x0, waiting for transfers between devices: 56.5 us -> none  [shards(): lax.all_gather(query_state[None], 'inner', axis=0, tiled=True)]
  transfers between devices with their start and end apart: 4 -> 3, of which waited for: 4 -> 3; matrix products, arithmetic and copies ran while one was open for 3% -> 3% of each run, Pallas kernels for 0% -> 0%
where the time goes in v1:
time: 790 us; the launch traced here: 787 us
  waiting for transfers between devices  489 us (62%)
  other arithmetic  126 us (16%)
  blocking collectives  100 us (13%)
  local copies, waits for them, and re-layouts  40.7 us (5%)
  matrix products  15.2 us (2%)
  between operations  14 us (2%)
    all_gather x2, waiting for transfers between devices, carried_in(): pieces = lax.all_gather(value, axis)  439 us
    all_to_all x1, blocking collectives, _move_skins(): lax.all_to_all(last, concat_axis=0, axis_name='inner', split_axis=0)  100 us
    select_n x62, other arithmetic, step(): return jnp.where(position < mine, longer, so_far)  98.5 us
    all_gather x1, waiting for transfers between devices, shards(): lax.all_gather(key_value_state[None], 'inner', axis=0, tiled=True)  50.3 us
    rev x1, local copies, waits for them, and re-layouts, carried_in(): pieces = pieces[::-1]  23 us
  transfers between devices with their start and end apart: 3, of which 3 were waited for; matrix products, arithmetic and copies ran while one was open for 3% of the time, Pallas kernels for 0%

profile of v1, /device:TPU:1, one launch (start us, length us, event | category | flops | bytes accessed | tf_op | source)
XLA Modules:
  0.0 786.6 jit_solution(8633407626280688745)
XLA Ops:
  13.7 100.2 %all_to_all.5 = f32[8,1,16,128,128]{4,3,2,1,0:T(8,128)} all-to-all(f32[8,1,16,128,128]{4,3,2,1,0:T(8,128)S(1)} %stack.3), channel_id=1, replica_groups=mesh['inner'=8,'outer'=32] {'inner'}, dimensions={0} | all-to-all | bytes 16777216 | tf_op jit(solution)/shard_map/all_to_all | solution.py:13
  114.0 5.2 reduce_sum.38
  121.3 2.0 copy.102
  126.1 5.5 fusion
  131.7 220.9 %all-gather.11.cloned.1.call-done = f32[512,128,128]{2,1,0:T(8,128)} async-done(((f32[16,128,128]{2,1,0:T(8,128)}), f32[512,128,128]{2,1,0:T(8,128)}) %all-gather.11.cloned.1.call-update) | async-done | bytes 33554448 | tf_op jit(solution)/shard_map/all_gather | solution.py:19
  352.6 23.0 %rev.3 = f32[32,16,128,128]{3,2,1,0:T(8,128)} reverse(f32[32,16,128,128]{3,2,1,0:T(8,128)} %bitcast.88), dimensions={0} | reverse | bytes 67108864 | tf_op jit(solution)/shard_map/rev | solution.py:21
  375.6 50.0 %while.29 = (s32[]{:T(128)}, f32[16,128,128]{2,1,0:T(8,128)S(1)}, s32[]{:T(128)}, f32[32,16,128,128]{3,2,1,0:T(8,128)}, s32[]{:T(128)}, /*index=5*/s32[]{:T(128)}) while((s32[]{:T(128)}, f32[16,128,128]{2,1,0:T(8,128)S(1)}, s32[]{:T(128)}, f32[32,16,128,128]{3,2,1,0:T(8,128)}, s32[]{:T(128)}, /*index=5*/s32[]{:T(128)}) %tuple.76), condition=%wide.region_6.7_spmd.clone, body=%wide.region_5.6_spmd.clone.sunk | while | flops 786436 | bytes 3145829 | solution.py:29
  378.8 1.6 add_select_fusion.5
  380.4 1.6 add_select_fusion.5
  382.0 1.6 add_select_fusion.5
  386.9 1.6 add_select_fusion.5
  388.5 1.6 add_select_fusion.5
  390.1 1.6 add_select_fusion.5
  393.3 1.6 add_select_fusion.5
  394.9 1.6 add_select_fusion.5
  396.5 1.6 add_select_fusion.5
  398.2 1.6 add_select_fusion.5
  401.4 1.6 add_select_fusion.5
  403.0 1.6 add_select_fusion.5
  404.6 1.6 add_select_fusion.5
  409.5 1.6 add_select_fusion.5
  411.1 1.6 add_select_fusion.5
  412.7 1.6 add_select_fusion.5
  417.5 1.6 add_select_fusion.5
  419.1 1.6 add_select_fusion.5
  420.7 1.6 add_select_fusion.5
  424.0 1.6 add_select_fusion.5
  426.9 1.9 fusion.6
  428.8 2.6 add_convert_fusion
  433.5 50.3 %all-gather.7.cloned.1.call-done = f32[128,128,128]{2,1,0:T(8,128)} async-done(((f32[16,128,128]{2,1,0:T(8,128)}), f32[128,128,128]{2,1,0:T(8,128)}) %all-gather.7.cloned.1.call-update) | async-done | bytes 8388624 | tf_op jit(solution)/shard_map/all_gather | solution.py:88
  483.8 6.1 select_reduce_fusion
  489.9 2.3 pad_maximum_fusion.3
  492.2 2.0 copy.82
  494.2 2.0 copy.87
  496.8 1.7 convolution_bitcast_fusion.1
  499.6 2.0 copy.88
  501.7 2.6 convolution_bitcast_fusion.3
  504.3 217.7 %all-gather.9.cloned.1.call-done = f32[512,128,128]{2,1,0:T(8,128)} async-done(((f32[16,128,128]{2,1,0:T(8,128)}), f32[512,128,128]{2,1,0:T(8,128)}) %all-gather.9.cloned.1.call-update) | async-done | bytes 33554448 | tf_op jit(solution)/shard_map/all_gather | solution.py:19
  722.1 50.0 %while.28 = (s32[]{:T(128)}, f32[16,128,128]{2,1,0:T(8,128)S(1)}, s32[]{:T(128)}, f32[32,16,128,128]{3,2,1,0:T(8,128)}, s32[]{:T(128)}, /*index=5*/s32[]{:T(128)}) while((s32[]{:T(128)}, f32[16,128,128]{2,1,0:T(8,128)S(1)}, s32[]{:T(128)}, f32[32,16,128,128]{3,2,1,0:T(8,128)}, s32[]{:T(128)}, /*index=5*/s32[]{:T(128)}) %tuple.88), condition=%wide.region_2.3_spmd.clone, body=%wide.region_1.2_spmd.clone.sunk | while | flops 786436 | bytes 3145829 | solution.py:29
  723.7 1.6 add_select_fusion.4
  725.3 1.6 add_select_fusion.4
  726.9 1.6 add_select_fusion.4
  730.1 1.6 add_select_fusion.4
  733.4 1.6 add_select_fusion.4
  736.6 1.6 add_select_fusion.4
  739.8 1.6 add_select_fusion.4
  743.1 1.6 add_select_fusion.4
  774.0 1.7 fusion.9
  (83 shorter events, 76.7 us)
Async XLA Ops:
  7.2 117.1 %copy-start = (bf16[128,2048]{1,0:T(8,128)(2,1)S(1)}, bf16[128,2048]{1,0:T(8,128)(2,1)}, u32[]{:S(2)}) copy-start(bf16[128,2048]{1,0:T(8,128)(2,1)} %param.11) | copy-start | bytes 1572868
  7.2 345.4 %all-gather.11.cloned.1.call-start = ((), (), s32[]{:S(2)}) async-start(), calls=%async_computation.3 | async-start | bytes 34603008 | tf_op jit(solution)/shard_map/all_gather | solution.py:19
  119.2 364.6 %all-gather.7.cloned.1.call-start = ((), (), s32[]{:S(2)}) async-start(), calls=%async_computation.1 | async-start | bytes 9437184 | tf_op jit(solution)/shard_map/all_gather | solution.py:88
  124.8 250.8 %copy-start.3 = (bf16[16,128,128]{2,1,0:T(8,128)(2,1)}, bf16[16,128,128]{2,1,0:T(8,128)(2,1)S(1)}, u32[]{:S(2)}) copy-start(bf16[16,128,128]{2,1,0:T(8,128)(2,1)S(1)} %fusion.12) | copy-start | bytes 1572868
  426.9 62.9 %copy-start.2 = (bf16[16,128,128]{2,1,0:T(8,128)(2,1)}, bf16[16,128,128]{2,1,0:T(8,128)(2,1)S(1)}, u32[]{:S(2)}) copy-start(bf16[16,128,128]{2,1,0:T(8,128)(2,1)S(1)} %add_convert_fusion.1) | copy-start | bytes 1572868
  433.2 288.9 %all-gather.9.cloned.1.call-start = ((), (), s32[]{:S(2)}) async-start(), calls=%async_computation.2 | async-start | bytes 34603008 | tf_op jit(solution)/shard_map/all_gather | solution.py:19
  496.7 1.8 copy-start.1
Sparse Core Ops, SparseCore 0:
  119.3 233.2 all-gather.10
  433.3 50.3 all-gather.6
  490.0 232.0 all-gather.8
